TPU v7x, 256 devices: a whole 4x4x8 slice. The times are simulated.
256 devices in a mesh: seq: 16 (over y_hi, z), batch: 16 (over y_lo, x, core).
Axes of the slice: x: 4, y: 4 (y_hi: 2, y_lo: 2; y = y_hi * 2 + y_lo), z: 8, core: 2. Of those that a mesh axis runs over, the one named last changes fastest.
Arguments:
- tokens: bfloat16 [16, 8192, 1536], P('batch', 'seq'), may hold values from -24 to 24
- filter_tap_weight: float32 [5, 1536], replicated, may hold values from -2.4 to 2.4
- norm_gain: float32 [1536], replicated, may hold values from 0.5 to 1.5
- query_weight: bfloat16 [1536, 512], replicated, may hold values from -4 to 4
- keyval_weight: bfloat16 [1536, 320], replicated, may hold values from -1 to 1
- head_weight: bfloat16 [768, 2, 384], replicated, may hold values from -0.21875 to 0.21875
- head_bias: float32 [2, 384], replicated, may hold values from -1 to 1
- exon_start: int32 [16, 32, 8], P('batch'), may hold values from 0 to 8191, as said below
- exon_end: int32 [16, 32, 8], P('batch'), may hold values from 0 to 8192, as said below
- gene_strand: int32 [16, 32], P('batch'), may hold values from 0 to 1
- gene_owner: int32 [16, 32, 1], P('batch'), may hold values from 0 to 15; in each aligned block of 32 rows (0 to 31, 32 to 63, ..., all dimensions but the last counted through in order) at most 4 rows name the same one
- gene_target: float32 [16, 16, 4, 384], P('batch'), may hold values from 0 to 4
Outputs:
- coverage: bfloat16 [16, 8192, 2, 384], P('batch', 'seq')
- gene_pred: float32 [16, 16, 4, 384], P('batch')
- head_grad: float32 [768, 2, 384], replicated
- bias_grad: float32 [2, 384], replicated
Inputs may be any that keep to these rules, and one draw needn't show every extreme that they name: `exon_start`: exons of a gene lie inside the window in increasing order without intersection, each of 1 to 4 bins; unused exon slots have start equal to end; every gene has at least one exon. `exon_end`: as exon_start. `gene_owner`: at most 4 genes of one window have the same owner.
All inputs are finite; a program needn't handle non-finite values.
Results may differ from a plain program's by a relative error of at most 0.025.
Values may be sent and summed in bfloat16 or wider, within the bound.
No kernel may reach another device: no remote copies, remote signals or barrier semaphores. Data moves between devices by JAX's collectives and lax.ppermute only.
A program may use at most 64 MiB of HBM per device.

v0:
```python
import math
import jax
import jax.numpy as jnp
from jax import lax
from jax.sharding import PartitionSpec as P

HEADS = 4
DK = 128
DV = 192
TRK = 384
FILTER_TAP_COUNT = 5
DILATION_STRIDE = 64


def extended(block, sides, width):
    for axis, dim in sides:
        count = lax.axis_size(axis)
        forward = [(i, i + 1) for i in range(count - 1)]
        backward = [(target, source) for source, target in forward]
        low = lax.ppermute(
            lax.slice_in_dim(block, block.shape[dim] - width, None, axis=dim), axis, forward
        )
        high = lax.ppermute(lax.slice_in_dim(block, 0, width, axis=dim), axis, backward)
        block = jnp.concatenate([low, block, high], axis=dim)
    return block


def make_fold(query_rows, scale_factor, state_now, pieces):
    key_rows, value_rows = pieces
    key_count = key_rows.shape[0]
    block_rows = math.gcd(key_count, 512)
    block_count = key_count // block_rows
    key_blocks = key_rows.reshape(block_count, block_rows, key_rows.shape[1])
    value_blocks = value_rows.reshape(block_count, block_rows, value_rows.shape[1])

    def one_block(running, block_pair):
        running_max, running_sum, weighted = running
        key_block, value_block = block_pair
        scores = (
            jnp.einsum("qhd,kd->qhk", query_rows, key_block, preferred_element_type=jnp.float32)
            * scale_factor
        )
        new_max = jnp.maximum(running_max, jnp.max(scores, axis=-1))
        shrink = jnp.exp(running_max - new_max)
        weights = jnp.exp(scores - new_max[..., None])
        running_sum = running_sum * shrink + jnp.sum(weights, axis=-1)
        weighted = weighted * shrink[..., None] + jnp.einsum(
            "qhk,kd->qhd",
            weights.astype(jnp.bfloat16),
            value_block,
            preferred_element_type=jnp.float32,
        )
        return ((new_max, running_sum, weighted), None)

    result_state, unused = lax.scan(one_block, state_now, (key_blocks, value_blocks))
    return result_state


def local(
    tokens,
    filter_tap_weight,
    norm_gain,
    query_weight,
    keyval_weight,
    head_weight,
    head_bias,
    exon_start,
    exon_end,
    gene_strand,
    gene_owner,
    gene_target,
):
    local_rows = tokens[0]
    window_row_count = local_rows.shape[0]
    dilation_reach_rows = FILTER_TAP_COUNT // 2 * DILATION_STRIDE
    zero_extended = extended(local_rows, (("seq", 0),), dilation_reach_rows)
    tap_total = local_rows.astype(jnp.float32)
    for filter_tap_index in range(FILTER_TAP_COUNT):
        tap_total = tap_total + filter_tap_weight[filter_tap_index] * zero_extended[
            filter_tap_index * DILATION_STRIDE : filter_tap_index * DILATION_STRIDE
            + window_row_count
        ].astype(jnp.float32)
    spread = jnp.mean(tap_total * tap_total, axis=-1, keepdims=True)
    normed = (tap_total * lax.rsqrt(spread + 1e-06) * norm_gain).astype(jnp.bfloat16)
    queries = jnp.dot(normed, query_weight, preferred_element_type=jnp.float32).astype(jnp.bfloat16)
    keyval = jnp.dot(normed, keyval_weight, preferred_element_type=jnp.float32)
    key_rows = keyval[:, :DK].astype(jnp.bfloat16)
    value_rows = keyval[:, DK:].astype(jnp.bfloat16)
    query_rows = queries.reshape(window_row_count, HEADS, DK)
    start_state = (
        jnp.full((window_row_count, HEADS), -jnp.inf, jnp.float32),
        jnp.zeros((window_row_count, HEADS), jnp.float32),
        jnp.zeros((window_row_count, HEADS, DV), jnp.float32),
    )
    running_max, running_sum, weighted = make_fold(
        query_rows,
        DK ** (-0.5),
        start_state,
        (
            lax.all_gather(key_rows, "seq", axis=0, tiled=True),
            lax.all_gather(value_rows, "seq", axis=0, tiled=True),
        ),
    )
    hidden_width = HEADS * DV
    attended = (
        (weighted / running_sum[..., None])
        .reshape(window_row_count, hidden_width)
        .astype(jnp.bfloat16)
    )
    logits = jnp.dot(
        attended, head_weight.reshape(hidden_width, 2 * TRK), preferred_element_type=jnp.float32
    ) + head_bias.reshape(2 * TRK)
    coverage = jax.nn.softplus(logits).astype(jnp.bfloat16).reshape(1, window_row_count, 2, TRK)
    positions = lax.axis_index("seq") * window_row_count + jnp.arange(
        window_row_count, dtype=jnp.int32
    )
    starts = exon_start[0]
    exon_stops = exon_end[0]
    inside = (positions[None, None, :] >= starts[:, :, None]) & (
        positions[None, None, :] < exon_stops[:, :, None]
    )
    counts = jnp.sum(inside.astype(jnp.int32), axis=1).astype(jnp.bfloat16)
    partial_pool = jnp.dot(counts, attended, preferred_element_type=jnp.float32)
    pooled = lax.psum(partial_pool.astype(jnp.bfloat16), "seq").astype(jnp.float32)
    length = jnp.sum((exon_stops - starts).astype(jnp.float32), axis=1)
    pooled = pooled / length[:, None]
    track_share = TRK
    weight_part = head_weight.astype(jnp.float32)
    per_strand = (
        jnp.einsum("gh,hst->gst", pooled, weight_part, precision=lax.Precision.HIGHEST)
        + head_bias[None]
    )
    strands = gene_strand[0]
    gene_logit = jnp.where(strands[:, None] == 0, per_strand[:, 0], per_strand[:, 1])
    owners = gene_owner[0, :, 0]
    gene_index = jnp.arange(owners.shape[0], dtype=jnp.int32)
    earlier = (owners[:, None] == owners[None, :]) & (gene_index[None, :] < gene_index[:, None])
    slot_rank = jnp.sum(earlier.astype(jnp.int32), axis=1)
    capacity = gene_target.shape[2]
    owner_count = lax.axis_size("batch")
    slot_index = owners * capacity + slot_rank
    slot_table = (
        jnp.arange(owner_count * capacity, dtype=jnp.int32)[:, None] == slot_index[None, :]
    ).astype(jnp.float32)
    outgoing = jnp.dot(
        slot_table, jax.nn.softplus(gene_logit), precision=lax.Precision.HIGHEST
    ).reshape(owner_count, capacity, track_share)
    arrived = lax.all_to_all(
        outgoing.astype(jnp.bfloat16), "batch", split_axis=0, concat_axis=0, tiled=True
    ).astype(outgoing.dtype)
    target_part = gene_target[0]
    gene_slope = (jnp.log1p(arrived) - target_part) / (1.0 + arrived)
    returned = lax.all_to_all(
        gene_slope.astype(jnp.bfloat16), "batch", split_axis=0, concat_axis=0, tiled=True
    ).astype(gene_slope.dtype)
    slope_rows = jnp.dot(
        slot_table.T,
        returned.reshape(owner_count * capacity, track_share),
        precision=lax.Precision.HIGHEST,
    )
    logit_grad = slope_rows * jax.nn.sigmoid(gene_logit)
    placed = jnp.stack(
        [
            jnp.where(strands[:, None] == 0, logit_grad, 0.0),
            jnp.where(strands[:, None] == 1, logit_grad, 0.0),
        ],
        axis=1,
    )
    window_head = jnp.einsum("gh,gst->hst", pooled, placed, precision=lax.Precision.HIGHEST)
    window_bias = jnp.sum(placed, axis=0)
    head_grad, bias_grad = (
        lax.psum(window_head.astype(jnp.bfloat16), "batch").astype(jnp.float32),
        lax.psum(window_bias.astype(jnp.bfloat16), "batch").astype(jnp.float32),
    )
    return (coverage, arrived[None], head_grad, bias_grad)


def solution(mesh):
    in_specs = (
        P("batch", "seq", None),
        P(),
        P(),
        P(),
        P(),
        P(),
        P(),
        P("batch", None, None),
        P("batch", None, None),
        P("batch", None),
        P("batch", None, None),
        P("batch", None, None, None),
    )
    out_specs = (P("batch", "seq", None, None), P("batch", None, None, None), P(), P())
    return jax.shard_map(local, mesh=mesh, in_specs=in_specs, out_specs=out_specs, check_vma=False)
```

profile of v0, /device:TPU:1, one launch (start us, length us, event | category | flops | bytes accessed | tf_op | source)
XLA Modules:
  0.0 601.8 jit_solution(12786762936528325310)
XLA Ops:
  8.6 4.4 collective-permute-start
  15.4 5.3 collective-permute-done
  20.7 4.2 collective-permute-done.1
  32.8 3.8 convolution_convert_fusion.1
  38.7 77.2 %all-gather.3.cloned.1.call-done = bf16[8192,128]{0,1:T(8,128)(2,1)} async-done(((bf16[512,128]{0,1:T(8,128)(2,1)}), bf16[8192,128]{0,1:T(8,128)(2,1)}) %all-gather.3.cloned.1.call-update) | async-done | bytes 2097168 | tf_op jit(solution)/shard_map/all_gather | solution.py:100
  115.9 4.1 copy.56
  120.0 90.2 %all-gather.5.cloned.1.call-done = bf16[8192,192]{0,1:T(8,128)(2,1)} async-done(((bf16[512,192]{0,1:T(8,128)(2,1)}), bf16[8192,192]{0,1:T(8,128)(2,1)}) %all-gather.5.cloned.1.call-update) | async-done | bytes 3145744 | tf_op jit(solution)/shard_map/all_gather | solution.py:101
  210.1 3.9 copy.64
  214.0 151.1 %while.15 = (s32[]{:T(128)}, f32[512,4]{0,1:T(4,128)S(1)}, f32[512,4]{0,1:T(4,128)S(1)}, f32[512,4,192]{0,2,1:T(8,128)S(1)}, bf16[16,512,128]{2,1,0:T(8,128)(2,1...) while((s32[]{:T(128)}, f32[512,4]{0,1:T(4,128)S(1)}, ...), condition=%wide.region_4.5_spmd.clone, body=%wide.region_1.4_spmd.clone.sunk | while | flops 680667136 | bytes 33490052 | solution.py:55
  214.0 3.7 bitcast_reduce_fusion.2
  223.5 3.8 bitcast_reduce_fusion.2
  232.9 3.8 bitcast_reduce_fusion.2
  242.4 3.8 bitcast_reduce_fusion.2
  251.8 3.8 bitcast_reduce_fusion.2
  261.3 3.8 bitcast_reduce_fusion.2
  270.7 3.8 bitcast_reduce_fusion.2
  280.2 3.8 bitcast_reduce_fusion.2
  289.6 3.8 bitcast_reduce_fusion.2
  299.1 3.8 bitcast_reduce_fusion.2
  308.5 3.8 bitcast_reduce_fusion.2
  318.0 3.8 bitcast_reduce_fusion.2
  327.4 3.8 bitcast_reduce_fusion.2
  336.8 3.8 bitcast_reduce_fusion.2
  346.3 3.8 bitcast_reduce_fusion.2
  355.7 3.8 bitcast_reduce_fusion.2
  366.6 58.8 %psum.21 = bf16[32,768]{1,0:T(8,128)(2,1)S(1)} all-reduce(bf16[32,768]{1,0:T(8,128)(2,1)S(1)} %convolution_convert_fusion.4), channel_id=1, replica_groups=mesh['seq'=16,'batch'=16] {'seq'}, use_global_device_ids=true, to_apply=%region_7.8 | all-reduce | flops 24576 | bytes 98304 | tf_op jit(solution)/shard_map/psum | solution.py:124
  427.9 30.3 %all_to_all.10 = bf16[16,4,384]{2,1,0:T(4,128)(2,1)S(1)} all-to-all(bf16[16,4,384]{2,1,0:T(4,128)(2,1)S(1)} %copy.53), channel_id=1, replica_groups=mesh['seq'=16,'batch'=16] {'batch'}, dimensions={0} | all-to-all | bytes 98304 | tf_op jit(solution)/shard_map/all_to_all | solution.py:148
  458.9 8.7 %all_to_all.11 = bf16[16,4,384]{2,1,0:T(4,128)(2,1)S(1)} all-to-all(bf16[16,4,384]{2,1,0:T(4,128)(2,1)S(1)} %fusion.35), channel_id=1, replica_groups=mesh['seq'=16,'batch'=16] {'batch'}, dimensions={0} | all-to-all | bytes 98304 | tf_op jit(solution)/shard_map/all_to_all | solution.py:153
  468.5 4.0 convolution_convert_fusion
  476.0 27.0 %psum.23 = bf16[2,384]{1,0:T(2,128)(2,1)S(1)} all-reduce(bf16[2,384]{1,0:T(2,128)(2,1)S(1)} %fusion.36), channel_id=1, replica_groups=mesh['seq'=16,'batch'=16] {'batch'}, use_global_device_ids=true, to_apply=%region_11.12 | all-reduce | flops 768 | bytes 3072 | tf_op jit(solution)/shard_map/psum | solution.py:173
  503.5 87.8 %all-reduce.2.cloned.1.call-done = bf16[768,2,384]{2,0,1:T(8,128)(2,1)} async-done(((bf16[768,2,384]{2,0,1:T(8,128)(2,1)}), bf16[768,2,384]{2,0,1:T(8,128)(2,1)}) %all-reduce.2.cloned.1.call-update) | async-done | bytes 1179664 | tf_op jit(solution)/shard_map/psum | solution.py:172
  591.4 3.9 copy.54
  (200 shorter events, 113.5 us)
Async XLA Ops:
  7.2 25.6 %copy-start = (bf16[1536,512]{1,0:T(8,128)(2,1)S(1)}, bf16[1536,512]{1,0:T(8,128)(2,1)}, u32[]{:S(2)}) copy-start(bf16[1536,512]{1,0:T(8,128)(2,1)} %param.17) | copy-start | bytes 4718596
  7.2 17.7 %copy-start.3 = (bf16[1,512,1536]{2,1,0:T(8,128)(2,1)S(1)}, bf16[1,512,1536]{2,1,0:T(8,128)(2,1)}, u32[]{:S(2)}) copy-start(bf16[1,512,1536]{2,1,0:T(8,128)(2,1)} %param.14) | copy-start | bytes 4718596
  7.2 108.7 %all-gather.3.cloned.1.call-start = ((), (), s32[]{:S(2)}) async-start(), calls=%async_computation.2 | async-start | bytes 2228224 | tf_op jit(solution)/shard_map/all_gather | solution.py:100
  8.6 12.1 %collective-permute-start = (bf16[128,1536]{1,0:T(8,128)(2,1)S(1)}, bf16[128,1536]{1,0:T(8,128)(2,1)S(1)}, u32[]{:S(2)}, u32[]{:S(2)}) collective-permute-start(bf16[128,1536]{1,0:T(8,128)(2,1)S(1)} %get-tuple-element.137), channel_id=1, source_target_pairs={{0,16},{16,32},{32,48},{48,64},{64,80},{80,96},{96,112},{112,128},... | collective-permute-start | bytes 1179656 | tf_op jit(solution)/shard_map/ppermute | solution.py:20
  13.0 11.9 %collective-permute-start.1 = (bf16[128,1536]{1,0:T(8,128)(2,1)S(1)}, bf16[128,1536]{1,0:T(8,128)(2,1)S(1)}, u32[]{:S(2)}, u32[]{:S(2)}) collective-permute-start(bf16[128,1536]{1,0:T(8,128)(2,1)S(1)} %get-tuple-element.138), channel_id=1, source_target_pairs={{16,0},{32,16},{48,32},{64,48},{80,64},{96,80},{112,96},{128,112},... | collective-permute-start | bytes 1179656 | tf_op jit(solution)/shard_map/ppermute | solution.py:23
  24.9 3.8 copy-start.7
  24.9 3.8 copy-start.18
  30.2 180.0 %all-gather.5.cloned.1.call-start = ((), (), s32[]{:S(2)}) async-start(), calls=%async_computation.3 | async-start | bytes 3342336 | tf_op jit(solution)/shard_map/all_gather | solution.py:101
  30.9 560.5 %all-reduce.2.cloned.1.call-start = ((), (), s32[]{:S(2)}) async-start(), calls=%async_computation.4 | async-start | bytes 2359296 | tf_op jit(solution)/shard_map/psum | solution.py:172
  217.8 3.4 copy-start.1
  227.2 3.4 copy-start.1
  236.7 3.4 copy-start.1
  246.1 3.4 copy-start.1
  255.6 3.4 copy-start.1
  265.0 3.4 copy-start.1
  274.5 3.4 copy-start.1
  283.9 3.4 copy-start.1
  293.4 3.4 copy-start.1
  302.8 3.4 copy-start.1
  312.3 3.4 copy-start.1
  321.7 3.4 copy-start.1
  331.2 3.4 copy-start.1
  340.6 3.4 copy-start.1
  350.1 3.4 copy-start.1
  359.5 3.4 copy-start.1
  365.2 60.2 %copy-start.19 = (f32[2,384]{1,0:T(2,128)S(1)}, f32[2,384]{1,0:T(2,128)}, u32[]{:S(2)}) copy-start(f32[2,384]{1,0:T(2,128)} %param.20) | copy-start | bytes 9220
  365.4 62.1 %copy-start.22 = (pred[32]{0:T(512)(128)(4,1)S(1)}, pred[32]{0:T(512)(128)(4,1)}, u32[]{:S(2)}) copy-start(pred[32]{0:T(512)(128)(4,1)} %get-tuple-element.142) | copy-start | bytes 100
  365.4 62.1 %copy-start.23 = (s32[32]{0:T(128)S(1)}, s32[32]{0:T(128)}, u32[]{:S(2)}) copy-start(s32[32]{0:T(128)} %multiply_add_fusion.1) | copy-start | bytes 388
  365.4 93.4 %copy-start.15 = (f32[1,16,4,384]{3,2,1,0:T(4,128)S(1)}, f32[1,16,4,384]{3,2,1,0:T(4,128)}, u32[]{:S(2)}) copy-start(f32[1,16,4,384]{3,2,1,0:T(4,128)} %param.25) | copy-start | bytes 294916
  425.4 42.4 %copy-start.14 = (bf16[32,768]{1,0:T(8,128)(2,1)}, bf16[32,768]{1,0:T(8,128)(2,1)S(1)}, u32[]{:S(2)}) copy-start(bf16[32,768]{1,0:T(8,128)(2,1)S(1)} %psum.21) | copy-start | bytes 147460
  425.4 47.1 %copy-start.6 = (bf16[768,2,384]{2,1,0:T(2,128)(2,1)S(1)}, bf16[768,2,384]{2,1,0:T(2,128)(2,1)}, u32[]{:S(2)}) copy-start(bf16[768,2,384]{2,1,0:T(2,128)(2,1)} %param.19) | copy-start | bytes 3538948
  468.4 4.3 copy-start.5
  (12 other events, 23.9 us)
Sparse Core Ops, SparseCore 0:
  30.3 85.5 all-gather.2
  118.4 91.7 all-gather.4
  472.6 118.7 all-reduce.1
where the time goes:
time: 603 us; the launch traced here: 602 us
  waiting for transfers between devices  265 us (44%)
  blocking collectives  125 us (21%)
  matrix products  108 us (18%)
  other arithmetic  54.5 us (9%)
  local copies, waits for them, and re-layouts  28.9 us (5%)
  between operations  14.1 us (2%)
    all_gather x1, waiting for transfers between devices, local(): lax.all_gather(value_rows, 'seq', axis=0, tiled=True)  90.2 us
    psum x1, waiting for transfers between devices, local(): lax.psum(window_head.astype(jnp.bfloat16), 'batch').astype(jnp.float32)  87.8 us
    all_gather x1, waiting for transfers between devices, local(): lax.all_gather(key_rows, 'seq', axis=0, tiled=True)  77.2 us
    dot_general x16, matrix products, one_block(): jnp.einsum('qhd,kd->qhk', query_rows, key_block, preferred_element_type=j...  60 us
    psum x1, blocking collectives, local(): lax.psum(partial_pool.astype(jnp.bfloat16), 'seq').astype(jnp.float32)  58.8 us
    reduce_sum x16, other arithmetic, one_block(): running_sum = running_sum * shrink + jnp.sum(weights, axis=-1)  48.9 us
    dot_general x16, matrix products, one_block(): jnp.einsum('qhk,kd->qhd', weights.astype(jnp.bfloat16), value_block, pref...  35.4 us
    all_to_all x1, blocking collectives, local(): lax.all_to_all(outgoing.astype(jnp.bfloat16), 'batch', split_axis=0, conc...  30.3 us
  transfers between devices with their start and end apart: 5, of which 5 were waited for; matrix products, arithmetic and copies ran while one was open for 3% of the time, Pallas kernels for 0%

commit v1 on v0

--- a/solution.py
+++ b/solution.py
@@ -10,6 +10,13 @@
 TRK = 384
 FILTER_TAP_COUNT = 5
 DILATION_STRIDE = 64
+
+
+def gather_over(x, name, d):
+    count = lax.axis_size(name)
+    blocks = jnp.stack([x for _ in range(count)])
+    blocks = lax.all_to_all(blocks, name, split_axis=0, concat_axis=0)
+    return jnp.concatenate(blocks, axis=d)
 
 
 def extended(block, sides, width):
@@ -96,10 +103,7 @@
         query_rows,
         DK ** (-0.5),
         start_state,
-        (
-            lax.all_gather(key_rows, "seq", axis=0, tiled=True),
-            lax.all_gather(value_rows, "seq", axis=0, tiled=True),
-        ),
+        (lax.all_gather(key_rows, "seq", axis=0, tiled=True), gather_over(value_rows, "seq", 0)),
     )
     hidden_width = HEADS * DV
     attended = (

time: 603 us -> 554 us (0.919)
  waiting for transfers between devices: 265 us -> 206 us
  starting transfers between devices: 5.81 us -> 16.4 us
    all_gather x1 -> x0, waiting for transfers between devices: 90.2 us -> none  [local(): lax.all_gather(value_rows, 'seq', axis=0, tiled=True)]
    all_gather x1, waiting for transfers between devices: 77.2 us -> 108 us  [local(): lax.all_gather(key_rows, 'seq', axis=0, tiled=True)]
    all_to_all x0 -> x1, starting transfers between devices: none -> 10.6 us  [gather_over(): blocks = lax.all_to_all(blocks, name, split_axis=0, concat_axis=0)]
  transfers between devices with their start and end apart: 5 -> 5, of which waited for: 5 -> 4; matrix products, arithmetic and copies ran while one was open for 3% -> 3% of each run, Pallas kernels for 0% -> 0%
where the time goes in v1:
time: 554 us; the launch traced here: 552 us
  waiting for transfers between devices  206 us (37%)
  blocking collectives  125 us (23%)
  matrix products  111 us (20%)
  other arithmetic  54.5 us (10%)
  local copies, waits for them, and re-layouts  25.3 us (5%)
  starting transfers between devices  16.4 us (3%)
  between operations  14.4 us (3%)
    all_gather x1, waiting for transfers between devices, local(): lax.all_gather(key_rows, 'seq', axis=0, tiled=True)  108 us
    psum x1, waiting for transfers between devices, local(): lax.psum(window_head.astype(jnp.bfloat16), 'batch').astype(jnp.float32)  87.9 us
    dot_general x16, matrix products, one_block(): jnp.einsum('qhd,kd->qhk', query_rows, key_block, preferred_element_type=j...  62.2 us
    psum x1, blocking collectives, local(): lax.psum(partial_pool.astype(jnp.bfloat16), 'seq').astype(jnp.float32)  59.6 us
    reduce_sum x16, other arithmetic, one_block(): running_sum = running_sum * shrink + jnp.sum(weights, axis=-1)  48.9 us
    dot_general x16, matrix products, one_block(): jnp.einsum('qhk,kd->qhd', weights.astype(jnp.bfloat16), value_block, pref...  35.4 us
    all_to_all x1, blocking collectives, local(): lax.all_to_all(outgoing.astype(jnp.bfloat16), 'batch', split_axis=0, conc...  29.6 us
    psum x1, blocking collectives, local(): lax.psum(window_bias.astype(jnp.bfloat16), 'batch').astype(jnp.float32)  27 us
  transfers between devices with their start and end apart: 5, of which 4 were waited for; matrix products, arithmetic and copies ran while one was open for 3% of the time, Pallas kernels for 0%

profile of v1, /device:TPU:1, one launch (start us, length us, event | category | flops | bytes accessed | tf_op | source)
XLA Modules:
  0.0 552.2 jit_solution(15619738844478998822)
XLA Ops:
  8.5 4.4 collective-permute-start
  15.3 5.3 collective-permute-done
  20.7 4.2 collective-permute-done.1
  30.6 10.6 %all-to-all-start = ((bf16[16,512,192]{1,2,0:T(8,128)(2,1)}), bf16[16,512,192]{1,2,0:T(8,128)(2,1)}, u32[]{:S(2)}, u32[]{:S(2)}) async-start(bf16[16,512,192]{1,2,0:T(8,128)(2,1)} %stack.8), calls=%async_computation | async-start | bytes 6291456 | tf_op jit(solution)/shard_map/all_to_all | solution.py:18
  43.8 3.8 convolution_convert_fusion.1
  49.6 108.2 %all-gather.2.cloned.1.call-done = bf16[8192,128]{0,1:T(8,128)(2,1)} async-done(((bf16[512,128]{0,1:T(8,128)(2,1)}), bf16[8192,128]{0,1:T(8,128)(2,1)}) %all-gather.2.cloned.1.call-update) | async-done | bytes 2097168 | tf_op jit(solution)/shard_map/all_gather | solution.py:106
  157.8 4.1 copy.52
  161.9 153.3 %while.15 = (s32[]{:T(128)}, f32[512,4]{0,1:T(4,128)S(1)}, f32[512,4]{0,1:T(4,128)S(1)}, f32[512,4,192]{0,2,1:T(8,128)S(1)}, bf16[16,512,128]{2,1,0:T(8,128)(2,1...) while((s32[]{:T(128)}, f32[512,4]{0,1:T(4,128)S(1)}, ...), condition=%wide.region_4.5_spmd.clone, body=%wide.region_1.4_spmd.clone.sunk | while | flops 680667136 | bytes 33490052 | solution.py:62
  161.9 3.9 bitcast_reduce_fusion.2
  165.8 3.1 fusion.81
  171.5 3.9 bitcast_reduce_fusion.2
  181.0 3.9 bitcast_reduce_fusion.2
  190.6 3.9 bitcast_reduce_fusion.2
  200.2 3.9 bitcast_reduce_fusion.2
  209.8 3.9 bitcast_reduce_fusion.2
  219.4 3.9 bitcast_reduce_fusion.2
  229.0 3.9 bitcast_reduce_fusion.2
  238.5 3.9 bitcast_reduce_fusion.2
  248.1 3.9 bitcast_reduce_fusion.2
  257.7 3.9 bitcast_reduce_fusion.2
  267.3 3.9 bitcast_reduce_fusion.2
  276.9 3.9 bitcast_reduce_fusion.2
  286.5 3.9 bitcast_reduce_fusion.2
  296.0 3.9 bitcast_reduce_fusion.2
  305.6 3.9 bitcast_reduce_fusion.2
  316.6 59.6 %psum.21 = bf16[32,768]{1,0:T(8,128)(2,1)S(1)} all-reduce(bf16[32,768]{1,0:T(8,128)(2,1)S(1)} %convolution_convert_fusion.4), channel_id=1, replica_groups=mesh['seq'=16,'batch'=16] {'seq'}, use_global_device_ids=true, to_apply=%region_7.8 | all-reduce | flops 24576 | bytes 98304 | tf_op jit(solution)/shard_map/psum | solution.py:128
  378.7 29.6 %all_to_all.15 = bf16[16,4,384]{2,1,0:T(4,128)(2,1)S(1)} all-to-all(bf16[16,4,384]{2,1,0:T(4,128)(2,1)S(1)} %copy.49), channel_id=1, replica_groups=mesh['seq'=16,'batch'=16] {'batch'}, dimensions={0} | all-to-all | bytes 98304 | tf_op jit(solution)/shard_map/all_to_all | solution.py:152
  409.0 8.7 %all_to_all.16 = bf16[16,4,384]{2,1,0:T(4,128)(2,1)S(1)} all-to-all(bf16[16,4,384]{2,1,0:T(4,128)(2,1)S(1)} %fusion.35), channel_id=1, replica_groups=mesh['seq'=16,'batch'=16] {'batch'}, dimensions={0} | all-to-all | bytes 98304 | tf_op jit(solution)/shard_map/all_to_all | solution.py:157
  418.5 4.0 convolution_convert_fusion
  426.1 27.0 %psum.23 = bf16[2,384]{1,0:T(2,128)(2,1)S(1)} all-reduce(bf16[2,384]{1,0:T(2,128)(2,1)S(1)} %fusion.36), channel_id=1, replica_groups=mesh['seq'=16,'batch'=16] {'batch'}, use_global_device_ids=true, to_apply=%region_11.12 | all-reduce | flops 768 | bytes 3072 | tf_op jit(solution)/shard_map/psum | solution.py:177
  453.6 87.9 %all-reduce.2.cloned.1.call-done = bf16[768,2,384]{2,0,1:T(8,128)(2,1)} async-done(((bf16[768,2,384]{2,0,1:T(8,128)(2,1)}), bf16[768,2,384]{2,0,1:T(8,128)(2,1)}) %all-reduce.2.cloned.1.call-update) | async-done | bytes 1179664 | tf_op jit(solution)/shard_map/psum | solution.py:176
  541.5 3.9 copy.50
  (199 shorter events, 110.8 us)
Async XLA Ops:
  7.2 36.6 %copy-start = (bf16[1536,512]{1,0:T(8,128)(2,1)S(1)}, bf16[1536,512]{1,0:T(8,128)(2,1)}, u32[]{:S(2)}) copy-start(bf16[1536,512]{1,0:T(8,128)(2,1)} %param.17) | copy-start | bytes 4718596
  7.2 17.6 %copy-start.3 = (bf16[1,512,1536]{2,1,0:T(8,128)(2,1)S(1)}, bf16[1,512,1536]{2,1,0:T(8,128)(2,1)}, u32[]{:S(2)}) copy-start(bf16[1,512,1536]{2,1,0:T(8,128)(2,1)} %param.14) | copy-start | bytes 4718596
  8.5 12.1 %collective-permute-start = (bf16[128,1536]{1,0:T(8,128)(2,1)S(1)}, bf16[128,1536]{1,0:T(8,128)(2,1)S(1)}, u32[]{:S(2)}, u32[]{:S(2)}) collective-permute-start(bf16[128,1536]{1,0:T(8,128)(2,1)S(1)} %get-tuple-element.137), channel_id=1, source_target_pairs={{0,16},{16,32},{32,48},{48,64},{64,80},{80,96},{96,112},{112,128},... | collective-permute-start | bytes 1179656 | tf_op jit(solution)/shard_map/ppermute | solution.py:27
  12.9 11.9 %collective-permute-start.1 = (bf16[128,1536]{1,0:T(8,128)(2,1)S(1)}, bf16[128,1536]{1,0:T(8,128)(2,1)S(1)}, u32[]{:S(2)}, u32[]{:S(2)}) collective-permute-start(bf16[128,1536]{1,0:T(8,128)(2,1)S(1)} %get-tuple-element.138), channel_id=1, source_target_pairs={{16,0},{32,16},{48,32},{64,48},{80,64},{96,80},{112,96},{128,112},... | collective-permute-start | bytes 1179656 | tf_op jit(solution)/shard_map/ppermute | solution.py:30
  30.6 11.4 %copy-start.17 = (s32[1,32,8]{1,2,0:T(8,128)S(1)}, s32[1,32,8]{1,2,0:T(8,128)}, u32[]{:S(2)}) copy-start(s32[1,32,8]{1,2,0:T(8,128)} %param.21) | copy-start | bytes 3076
  30.6 11.5 %copy-start.16 = (s32[1,32,8]{1,2,0:T(8,128)S(1)}, s32[1,32,8]{1,2,0:T(8,128)}, u32[]{:S(2)}) copy-start(s32[1,32,8]{1,2,0:T(8,128)} %param.22) | copy-start | bytes 3076
  30.6 11.6 %copy-start.21 = (s32[1,32,1]{1,2,0:T(1,128)S(1)}, s32[1,32,1]{1,2,0:T(1,128)}, u32[]{:S(2)}) copy-start(s32[1,32,1]{1,2,0:T(1,128)} %param.24) | copy-start | bytes 388
  30.6 12.1 %copy-start.20 = (s32[1,32]{1,0:T(1,128)S(1)}, s32[1,32]{1,0:T(1,128)}, u32[]{:S(2)}) copy-start(s32[1,32]{1,0:T(1,128)} %param.23) | copy-start | bytes 388
  30.6 131.3 %all-to-all-start = ((bf16[16,512,192]{1,2,0:T(8,128)(2,1)}), bf16[16,512,192]{1,2,0:T(8,128)(2,1)}, u32[]{:S(2)}, u32[]{:S(2)}) async-start(bf16[16,512,192]{1,2,0:T(8,128)(2,1)} %stack.8), calls=%async_computation | async-start | bytes 6291456 | tf_op jit(solution)/shard_map/all_to_all | solution.py:18
  41.2 116.6 %all-gather.2.cloned.1.call-start = ((), (), s32[]{:S(2)}) async-start(), calls=%async_computation.3 | async-start | bytes 2228224 | tf_op jit(solution)/shard_map/all_gather | solution.py:106
  41.9 499.6 %all-reduce.2.cloned.1.call-start = ((), (), s32[]{:S(2)}) async-start(), calls=%async_computation.4 | async-start | bytes 2359296 | tf_op jit(solution)/shard_map/psum | solution.py:176
  165.8 3.4 copy-start.1
  175.3 3.4 copy-start.1
  184.9 3.4 copy-start.1
  194.5 3.4 copy-start.1
  204.1 3.4 copy-start.1
  213.7 3.4 copy-start.1
  223.3 3.4 copy-start.1
  232.8 3.4 copy-start.1
  242.4 3.4 copy-start.1
  252.0 3.4 copy-start.1
  261.6 3.4 copy-start.1
  271.2 3.4 copy-start.1
  280.8 3.4 copy-start.1
  290.3 3.4 copy-start.1
  315.2 61.1 %copy-start.19 = (f32[2,384]{1,0:T(2,128)S(1)}, f32[2,384]{1,0:T(2,128)}, u32[]{:S(2)}) copy-start(f32[2,384]{1,0:T(2,128)} %param.20) | copy-start | bytes 9220
  315.4 63.0 %copy-start.22 = (pred[32]{0:T(512)(128)(4,1)S(1)}, pred[32]{0:T(512)(128)(4,1)}, u32[]{:S(2)}) copy-start(pred[32]{0:T(512)(128)(4,1)} %get-tuple-element.142) | copy-start | bytes 100
  315.4 62.9 %copy-start.23 = (s32[32]{0:T(128)S(1)}, s32[32]{0:T(128)}, u32[]{:S(2)}) copy-start(s32[32]{0:T(128)} %multiply_add_fusion.1) | copy-start | bytes 388
  315.5 93.5 %copy-start.15 = (f32[1,16,4,384]{3,2,1,0:T(4,128)S(1)}, f32[1,16,4,384]{3,2,1,0:T(4,128)}, u32[]{:S(2)}) copy-start(f32[1,16,4,384]{3,2,1,0:T(4,128)} %param.25) | copy-start | bytes 294916
  376.2 41.7 %copy-start.14 = (bf16[32,768]{1,0:T(8,128)(2,1)}, bf16[32,768]{1,0:T(8,128)(2,1)S(1)}, u32[]{:S(2)}) copy-start(bf16[32,768]{1,0:T(8,128)(2,1)S(1)} %psum.21) | copy-start | bytes 147460
  376.3 46.3 %copy-start.6 = (bf16[768,2,384]{2,1,0:T(2,128)(2,1)S(1)}, bf16[768,2,384]{2,1,0:T(2,128)(2,1)}, u32[]{:S(2)}) copy-start(bf16[768,2,384]{2,1,0:T(2,128)(2,1)} %param.19) | copy-start | bytes 3538948
  418.5 4.3 copy-start.5
  (12 other events, 24.5 us)
Sparse Core Ops, SparseCore 0:
  45.1 112.7 all-gather.1
  422.7 118.7 all-reduce.1
